TPU v7x, 32 devices: a whole 2x2x4 slice. The times are simulated.
32 devices in a mesh: dp: 8 (over z, x), shard: 4 (over y, core).
Axes of the slice: x: 2, y: 2, z: 4, core: 2. Of those that a mesh axis runs over, the one named last changes fastest.
Arguments:
- target: bfloat16 [32, 1024, 512], P(('dp', 'shard')), may hold values from -6 to 6
- memory: bfloat16 [32, 1024, 512], P(('dp', 'shard')), may hold values from -6 to 6
- cotangent: bfloat16 [32, 1024, 512], P(('dp', 'shard')), may hold values from -6 to 6
- target_lengths: int32 [32, 24], P(('dp', 'shard')), may hold values from 1 to 512, 1024 in all within a row
- source_lengths: int32 [32, 24], P(('dp', 'shard')), may hold values from 1 to 512, 1024 in all within a row
- inward_master: float32 [1572864], P(('dp', 'shard')), may hold values from -0.25 to 0.25
- inward_mean: float32 [1572864], P(('dp', 'shard')), may hold values from -320 to 320
- inward_square: float32 [1572864], P(('dp', 'shard')), may hold values from 327.68 to 32768
- outward_master: float32 [524288], P(('dp', 'shard')), may hold values from -0.75 to 0.75
- outward_mean: float32 [524288], P(('dp', 'shard')), may hold values from -320 to 320
- outward_square: float32 [524288], P(('dp', 'shard')), may hold values from 327.68 to 32768
- expand_master: float32 [1048576], P(('dp', 'shard')), may hold values from -0.25 to 0.25
- expand_mean: float32 [1048576], P(('dp', 'shard')), may hold values from -320 to 320
- expand_square: float32 [1048576], P(('dp', 'shard')), may hold values from 327.68 to 32768
- shrink_master: float32 [1048576], P(('dp', 'shard')), may hold values from -0.125 to 0.125
- shrink_mean: float32 [1048576], P(('dp', 'shard')), may hold values from -320 to 320
- shrink_square: float32 [1048576], P(('dp', 'shard')), may hold values from 327.68 to 32768
- norms_master: float32 [3072], P(('dp', 'shard')), may hold values from -0.5 to 1.3, as said below
- norms_mean: float32 [3072], P(('dp', 'shard')), may hold values from -320 to 320
- norms_square: float32 [3072], P(('dp', 'shard')), may hold values from 327.68 to 32768
Outputs:
- result: bfloat16 [32, 1024, 512], P(('dp', 'shard'))
- target_grad: float32 [32, 1024, 512], P(('dp', 'shard'))
- memory_grad: float32 [32, 1024, 512], P(('dp', 'shard'))
- change_inward: float32 [1572864], P(('dp', 'shard'))
- mean_inward: float32 [1572864], P(('dp', 'shard'))
- summed_inward: float32 [1572864], P(('dp', 'shard'))
- change_outward: float32 [524288], P(('dp', 'shard'))
- mean_outward: float32 [524288], P(('dp', 'shard'))
- summed_outward: float32 [524288], P(('dp', 'shard'))
- change_expand: float32 [1048576], P(('dp', 'shard'))
- mean_expand: float32 [1048576], P(('dp', 'shard'))
- summed_expand: float32 [1048576], P(('dp', 'shard'))
- change_shrink: float32 [1048576], P(('dp', 'shard'))
- mean_shrink: float32 [1048576], P(('dp', 'shard'))
- summed_shrink: float32 [1048576], P(('dp', 'shard'))
- change_norms: float32 [3072], P(('dp', 'shard'))
- mean_norms: float32 [3072], P(('dp', 'shard'))
- summed_norms: float32 [3072], P(('dp', 'shard'))
Inputs may be any that keep to these rules, and one draw needn't show every extreme that they name: `target_lengths`: in each row the 24 lengths sum to 1024; the last entry is padding, the others are sentences; target sentence i is the translation of source sentence i. `source_lengths`: as target_lengths, for the source side. `norms_master`: the first 1536 entries are gains, the others biases.
All inputs are finite; a program needn't handle non-finite values.
Results may differ from a plain program's by a relative error of at most 0.015.
The roundings to bfloat16 on the way count: a program that leaves them out, or rounds other values in their place, can miss the bound.
Values may be sent and summed in bfloat16 or wider, within the bound.
A program may use at most 192 MiB of HBM per device.

v0:
```python
import jax
import jax.numpy as jnp
from jax import lax
from jax.sharding import PartitionSpec as P

D = 512
HEADS = 8
HD = 64
FF = 2048
ROW = 1024
SEGS = 24
STEP = 10
learn_rate = 0.001
beta_one = 0.9
beta_two = 0.999


def matmul(left_mat, right_mat):
    return jnp.dot(left_mat, right_mat, preferred_element_type=jnp.float32)


def left_dot(left_mat, right_mat):
    return lax.dot_general(
        left_mat, right_mat, (((0,), (0,)), ((), ())), preferred_element_type=jnp.float32
    )


def right_dot(left_mat, right_mat):
    return lax.dot_general(
        left_mat, right_mat, (((1,), (1,)), ((), ())), preferred_element_type=jnp.float32
    )


def layer_norm(residual, norm_gain, norm_bias):
    centered = residual - jnp.mean(residual, -1, keepdims=True)
    spread = jnp.mean(centered * centered, -1, keepdims=True)
    return centered * lax.rsqrt(spread + 1e-05) * norm_gain + norm_bias


def segments(lengths):
    ends = jnp.cumsum(lengths, axis=-1)
    places = jnp.arange(ROW, dtype=jnp.int32)
    return jnp.sum((places[None, :, None] >= ends[:, None, :]).astype(jnp.int32), -1)


def pair_mask(query_seg, key_seg, row_start, causal):
    allowed = query_seg[:, None] == key_seg[None, :]
    if causal:
        query_pos = row_start + jnp.arange(query_seg.shape[0], dtype=jnp.int32)
        key_pos = jnp.arange(key_seg.shape[0], dtype=jnp.int32)
        allowed = allowed & (key_pos[None, :] <= query_pos[:, None])
    return allowed


def attend(queries, keys, values, query_seg, key_seg, causal):
    block_rows = min(512, queries.shape[1])
    block_count = queries.shape[1] // block_rows
    score_scale = queries.shape[3] ** (-0.5)

    def one_row(row_items):
        q_row, k_row, v_row, qs_row, ks_row = row_items

        def one_block(block_index):
            row_start = block_index * block_rows
            q_block = lax.dynamic_slice_in_dim(q_row, row_start, block_rows, 0)
            seg_block = lax.dynamic_slice_in_dim(qs_row, row_start, block_rows, 0)
            scores = (
                jnp.einsum("qhd,khd->hqk", q_block, k_row, preferred_element_type=jnp.float32)
                * score_scale
            )
            allowed = pair_mask(seg_block, ks_row, row_start, causal)
            scores = jnp.where(allowed[None], scores, -1000000000.0)
            row_peak = jnp.max(scores, -1, keepdims=True)
            raised = jnp.exp(scores - row_peak)
            row_total = jnp.sum(raised, -1, keepdims=True)
            probs = (raised / row_total).astype(jnp.bfloat16)
            context = jnp.einsum("hqk,khd->qhd", probs, v_row, preferred_element_type=jnp.float32)
            return (context, row_peak[..., 0] + jnp.log(row_total[..., 0]))

        context, logsum = lax.map(one_block, jnp.arange(block_count, dtype=jnp.int32))
        return (context.reshape(-1, q_row.shape[1] * q_row.shape[2]), logsum)

    return lax.map(one_row, (queries, keys, values, query_seg, key_seg))


def attend_back(queries, keys, values, logsum, grad_ctx, query_seg, key_seg, causal):
    block_rows = min(512, queries.shape[1])
    block_count = queries.shape[1] // block_rows
    score_scale = queries.shape[3] ** (-0.5)

    def one_row(row_items):
        q_row, k_row, v_row, ls_row, g_row, qs_row, ks_row = row_items

        def one_block(carry, block_index):
            grad_keys, grad_values = carry
            row_start = block_index * block_rows
            q_block = lax.dynamic_slice_in_dim(q_row, row_start, block_rows, 0)
            g_block = lax.dynamic_slice_in_dim(g_row, row_start, block_rows, 0)
            seg_block = lax.dynamic_slice_in_dim(qs_row, row_start, block_rows, 0)
            ls_block = lax.dynamic_index_in_dim(ls_row, block_index, 0, keepdims=False)
            scores = (
                jnp.einsum("qhd,khd->hqk", q_block, k_row, preferred_element_type=jnp.float32)
                * score_scale
            )
            allowed = pair_mask(seg_block, ks_row, row_start, causal)
            probs = jnp.where(allowed[None], jnp.exp(scores - ls_block[..., None]), 0.0)
            grad_probs = jnp.einsum(
                "qhd,khd->hqk", g_block, v_row, preferred_element_type=jnp.float32
            )
            inner = jnp.sum(probs * grad_probs, -1, keepdims=True)
            grad_scores = (probs * (grad_probs - inner) * score_scale).astype(jnp.bfloat16)
            grad_query = jnp.einsum(
                "hqk,khd->qhd", grad_scores, k_row, preferred_element_type=jnp.float32
            )
            grad_keys = grad_keys + jnp.einsum(
                "hqk,qhd->khd", grad_scores, q_block, preferred_element_type=jnp.float32
            )
            grad_values = grad_values + jnp.einsum(
                "hqk,qhd->khd",
                probs.astype(jnp.bfloat16),
                g_block,
                preferred_element_type=jnp.float32,
            )
            return ((grad_keys, grad_values), grad_query)

        empty = jnp.zeros(k_row.shape, jnp.float32)
        (grad_keys, grad_values), grad_query = lax.scan(
            one_block, (empty, empty), jnp.arange(block_count, dtype=jnp.int32)
        )
        return (grad_query.reshape(q_row.shape), grad_keys, grad_values)

    return lax.map(one_row, (queries, keys, values, logsum, grad_ctx, query_seg, key_seg))


def unpack(inward_all, outward_all, norms_all, expand_all, shrink_all):
    norm_par = norms_all.reshape(2, 3, D).astype(jnp.float32)
    return (
        inward_all.reshape(6, D, D),
        outward_all.reshape(2, D, D),
        expand_all.reshape(D, FF),
        shrink_all.reshape(FF, D),
        norm_par[0],
        norm_par[1],
    )


def adam_step(mean_old, square_old, grad_share):
    mean_new = beta_one * mean_old + (1.0 - beta_one) * grad_share
    square_new = beta_two * square_old + (1.0 - beta_two) * grad_share * grad_share
    steps_float = float(STEP)
    mean_hat = mean_new / (1.0 - beta_one**steps_float)
    square_hat = square_new / (1.0 - beta_two**steps_float)
    change = -learn_rate * mean_hat / (jnp.sqrt(square_hat) + 1e-08)
    return (change, mean_new, grad_share)


def body(
    target,
    memory,
    cotangent,
    target_lengths,
    source_lengths,
    inward_master,
    inward_mean,
    inward_square,
    outward_master,
    outward_mean,
    outward_square,
    expand_master,
    expand_mean,
    expand_square,
    shrink_master,
    shrink_mean,
    shrink_square,
    norms_master,
    norms_mean,
    norms_square,
):
    row_count = target.shape[0]
    inward_low = inward_master.astype(jnp.bfloat16)
    outward_low = outward_master.astype(jnp.bfloat16)
    expand_low = expand_master.astype(jnp.bfloat16)
    shrink_low = shrink_master.astype(jnp.bfloat16)
    norms_low = norms_master.astype(jnp.bfloat16)
    inward_all, outward_all, norms_all = (
        lax.all_gather(inward_low, ("dp", "shard"), axis=0, tiled=True),
        lax.all_gather(outward_low, ("dp", "shard"), axis=0, tiled=True),
        lax.all_gather(norms_low, ("dp", "shard"), axis=0, tiled=True),
    )
    expand_all, shrink_all = (
        lax.all_gather(expand_low, ("dp", "shard"), axis=0, tiled=True),
        lax.all_gather(shrink_low, ("dp", "shard"), axis=0, tiled=True),
    )
    w_in, w_out, w_up, w_down, gains, biases = unpack(
        inward_all, outward_all, norms_all, expand_all, shrink_all
    )
    target_seg = segments(target_lengths)
    source_seg = segments(source_lengths)
    live_rows = (target_seg < SEGS - 1).astype(jnp.float32).reshape(-1, 1)

    def heads(values_flat):
        return values_flat.reshape(row_count, ROW, HEADS, HD)

    tokens = target.reshape(-1, D)
    source = memory.reshape(-1, D)
    query_one = matmul(tokens, w_in[0]).astype(jnp.bfloat16)
    key_one = matmul(tokens, w_in[1]).astype(jnp.bfloat16)
    value_one = matmul(tokens, w_in[2]).astype(jnp.bfloat16)
    ctx_raw, logsum_one = attend(
        heads(query_one), heads(key_one), heads(value_one), target_seg, target_seg, True
    )
    ctx_one = ctx_raw.reshape(-1, D).astype(jnp.bfloat16)
    resid_one = tokens.astype(jnp.float32) + matmul(ctx_one, w_out[0])
    hidden_one = layer_norm(resid_one, gains[0], biases[0])
    hidden_low = hidden_one.astype(jnp.bfloat16)
    query_two = matmul(hidden_low, w_in[3]).astype(jnp.bfloat16)
    key_two = matmul(source, w_in[4]).astype(jnp.bfloat16)
    value_two = matmul(source, w_in[5]).astype(jnp.bfloat16)
    ctx_raw, logsum_two = attend(
        heads(query_two), heads(key_two), heads(value_two), target_seg, source_seg, False
    )
    ctx_two = ctx_raw.reshape(-1, D).astype(jnp.bfloat16)
    resid_two = hidden_one + matmul(ctx_two, w_out[1])
    hidden_two = layer_norm(resid_two, gains[1], biases[1])
    second_low = hidden_two.astype(jnp.bfloat16)
    pre_act = matmul(second_low, w_up)
    activated = jax.nn.silu(pre_act).astype(jnp.bfloat16)
    resid_three = hidden_two + matmul(activated, w_down)
    output = layer_norm(resid_three, gains[2], biases[2])
    inward_back, outward_back, norms_back, expand_back, shrink_back = (
        lax.all_gather(inward_low, ("dp", "shard"), axis=0, tiled=True),
        lax.all_gather(outward_low, ("dp", "shard"), axis=0, tiled=True),
        lax.all_gather(norms_low, ("dp", "shard"), axis=0, tiled=True),
        lax.all_gather(expand_low, ("dp", "shard"), axis=0, tiled=True),
        lax.all_gather(shrink_low, ("dp", "shard"), axis=0, tiled=True),
    )
    w_in, w_out, w_up, w_down, gains, biases = unpack(
        inward_back, outward_back, norms_back, expand_back, shrink_back
    )
    seed = cotangent.reshape(-1, D).astype(jnp.float32) * live_rows
    _, pull_three = jax.vjp(layer_norm, resid_three, gains[2], biases[2])
    grad_three, gain_three, bias_three = pull_three(seed)
    grad_out = grad_three.astype(jnp.bfloat16)
    grad_shrink = left_dot(activated, grad_out)
    grad_act = right_dot(grad_out, w_down)
    _, pull_act = jax.vjp(jax.nn.silu, pre_act)
    grad_pre = pull_act(grad_act)[0].astype(jnp.bfloat16)
    grad_expand = left_dot(second_low, grad_pre)
    grad_hidden_two = grad_three + right_dot(grad_pre, w_up)
    _, pull_two = jax.vjp(layer_norm, resid_two, gains[1], biases[1])
    grad_two, gain_two, bias_two = pull_two(grad_hidden_two)
    branch_two = grad_two.astype(jnp.bfloat16)
    grad_wo_two = left_dot(ctx_two, branch_two)
    grad_ctx_two = right_dot(branch_two, w_out[1]).astype(jnp.bfloat16)
    dq_two, dk_two, dv_two = attend_back(
        heads(query_two),
        heads(key_two),
        heads(value_two),
        logsum_two,
        heads(grad_ctx_two),
        target_seg,
        source_seg,
        False,
    )
    dq_two = dq_two.reshape(-1, D).astype(jnp.bfloat16)
    dk_two = dk_two.reshape(-1, D).astype(jnp.bfloat16)
    dv_two = dv_two.reshape(-1, D).astype(jnp.bfloat16)
    grad_wq_two = left_dot(hidden_low, dq_two)
    grad_wk_two = left_dot(source, dk_two)
    grad_wv_two = left_dot(source, dv_two)
    memory_grad = right_dot(dk_two, w_in[4]) + right_dot(dv_two, w_in[5])
    grad_hidden_one = grad_two + right_dot(dq_two, w_in[3])
    _, pull_one = jax.vjp(layer_norm, resid_one, gains[0], biases[0])
    grad_one, gain_one, bias_one = pull_one(grad_hidden_one)
    branch_one = grad_one.astype(jnp.bfloat16)
    grad_wo_one = left_dot(ctx_one, branch_one)
    grad_ctx_one = right_dot(branch_one, w_out[0]).astype(jnp.bfloat16)
    dq_one, dk_one, dv_one = attend_back(
        heads(query_one),
        heads(key_one),
        heads(value_one),
        logsum_one,
        heads(grad_ctx_one),
        target_seg,
        target_seg,
        True,
    )
    dq_one = dq_one.reshape(-1, D).astype(jnp.bfloat16)
    dk_one = dk_one.reshape(-1, D).astype(jnp.bfloat16)
    dv_one = dv_one.reshape(-1, D).astype(jnp.bfloat16)
    grad_wq_one = left_dot(tokens, dq_one)
    grad_wk_one = left_dot(tokens, dk_one)
    grad_wv_one = left_dot(tokens, dv_one)
    target_grad = (
        grad_one
        + right_dot(dq_one, w_in[0])
        + right_dot(dk_one, w_in[1])
        + right_dot(dv_one, w_in[2])
    )
    grad_inward = jnp.stack(
        [grad_wq_one, grad_wk_one, grad_wv_one, grad_wq_two, grad_wk_two, grad_wv_two]
    ).reshape(-1)
    grad_outward = jnp.stack([grad_wo_one, grad_wo_two]).reshape(-1)
    grad_norms = jnp.stack(
        [jnp.stack([gain_one, gain_two, gain_three]), jnp.stack([bias_one, bias_two, bias_three])]
    ).reshape(-1)
    inward_share, outward_share, norms_share, expand_share, shrink_share = (
        lax.psum_scatter(grad_inward, ("dp", "shard"), scatter_dimension=0, tiled=True),
        lax.psum_scatter(grad_outward, ("dp", "shard"), scatter_dimension=0, tiled=True),
        lax.psum_scatter(grad_norms, ("dp", "shard"), scatter_dimension=0, tiled=True),
        lax.psum_scatter(grad_expand.reshape(-1), ("dp", "shard"), scatter_dimension=0, tiled=True),
        lax.psum_scatter(grad_shrink.reshape(-1), ("dp", "shard"), scatter_dimension=0, tiled=True),
    )
    in_c, in_m, in_g = adam_step(inward_mean, inward_square, inward_share)
    out_c, out_m, out_g = adam_step(outward_mean, outward_square, outward_share)
    up_c, up_m, up_g = adam_step(expand_mean, expand_square, expand_share)
    down_c, down_m, down_g = adam_step(shrink_mean, shrink_square, shrink_share)
    norm_c, norm_m, norm_g = adam_step(norms_mean, norms_square, norms_share)
    shape_rows = (row_count, ROW, D)
    return (
        output.astype(jnp.bfloat16).reshape(shape_rows),
        target_grad.reshape(shape_rows),
        memory_grad.reshape(shape_rows),
        in_c,
        in_m,
        in_g,
        out_c,
        out_m,
        out_g,
        up_c,
        up_m,
        up_g,
        down_c,
        down_m,
        down_g,
        norm_c,
        norm_m,
        norm_g,
    )


def solution(mesh):
    return jax.shard_map(
        body,
        mesh=mesh,
        in_specs=(
            P(("dp", "shard"), None, None),
            P(("dp", "shard"), None, None),
            P(("dp", "shard"), None, None),
            P(("dp", "shard"), None),
            P(("dp", "shard"), None),
            P(("dp", "shard")),
            P(("dp", "shard")),
            P(("dp", "shard")),
            P(("dp", "shard")),
            P(("dp", "shard")),
            P(("dp", "shard")),
            P(("dp", "shard")),
            P(("dp", "shard")),
            P(("dp", "shard")),
            P(("dp", "shard")),
            P(("dp", "shard")),
            P(("dp", "shard")),
            P(("dp", "shard")),
            P(("dp", "shard")),
            P(("dp", "shard")),
        ),
        out_specs=(
            P(("dp", "shard"), None, None),
            P(("dp", "shard"), None, None),
            P(("dp", "shard"), None, None),
            P(("dp", "shard")),
            P(("dp", "shard")),
            P(("dp", "shard")),
            P(("dp", "shard")),
            P(("dp", "shard")),
            P(("dp", "shard")),
            P(("dp", "shard")),
            P(("dp", "shard")),
            P(("dp", "shard")),
            P(("dp", "shard")),
            P(("dp", "shard")),
            P(("dp", "shard")),
            P(("dp", "shard")),
            P(("dp", "shard")),
            P(("dp", "shard")),
        ),
        check_vma=False,
    )
```

profile of v0, /device:TPU:0, one launch (start us, length us, event | category | flops | bytes accessed | tf_op | source)
XLA Modules:
  0.0 1016.5 jit_solution(18071916766514258898)
XLA Ops:
  17.8 42.1 %all-reduce = bf16[3072]{0:T(1024)(128)(2,1)S(1)} all-reduce(bf16[3072]{0:T(1024)(128)(2,1)S(1)} %dynamic-update-slice), channel_id=1, replica_groups=mesh['dp'=8,'shard'=4] {'dp','shard'}, use_global_device_ids=true, to_apply=%add | all-reduce | flops 3072 | bytes 12288
  64.1 4.2 all-gather.7.cloned.1.call-done
  71.8 55.1 %all-gather.9.cloned.1.call-done = bf16[1048576]{0:T(1024)(128)(2,1)} async-done(((bf16[32768]{0:T(1024)(128)(2,1)}), bf16[1048576]{0:T(1024)(128)(2,1)}) %all-gather.9.cloned.1.call-update) | async-done | bytes 2097168 | tf_op jit(solution)/shard_map/all_gather | solution.py:191
  126.9 4.2 reshape.655
  131.1 54.6 %all-gather.11.cloned.1.call-done = bf16[1048576]{0:T(1024)(128)(2,1)} async-done(((bf16[32768]{0:T(1024)(128)(2,1)}), bf16[1048576]{0:T(1024)(128)(2,1)}) %all-gather.11.cloned.1.call-update) | async-done | bytes 2097168 | tf_op jit(solution)/shard_map/all_gather | solution.py:192
  185.6 4.4 reshape.656
  190.0 56.9 %all-gather.5.cloned.1.call-done = bf16[1572864]{0:T(1024)(128)(2,1)} async-done(((bf16[49152]{0:T(1024)(128)(2,1)}), bf16[1572864]{0:T(1024)(128)(2,1)}) %all-gather.5.cloned.1.call-update) | async-done | bytes 3145744 | tf_op jit(solution)/shard_map/all_gather | solution.py:186
  246.9 3.0 fusion.159
  257.1 3.1 convolution_convert_fusion.7
  267.0 33.5 %while.96 = (s32[]{:T(128)}, bf16[2,512,8,64]{1,3,2,0:T(8,128)(2,1)}, f32[2,8,512]{2,1,0:T(8,128)S(1)}, s32[2]{0:T(128)S(1)}, s32[1024]{0:T(1024)S(1)}, /*index=...) while((s32[]{:T(128)}, ...), condition=%wide.region_5.6_spmd, body=%wide.region_2.0_spmd.sunk | while | flops 1125642752 | bytes 64633092 | solution.py:80
  269.2 4.1 fusion.257
  273.3 4.2 fusion.258
  277.5 5.4 fusion.259
  285.8 4.1 fusion.257
  289.9 4.2 fusion.258
  294.2 5.4 fusion.259
  300.5 3.1 copy.79
  309.4 41.3 %while.97 = (s32[]{:T(128)}, bf16[2,512,8,64]{1,3,2,0:T(8,128)(2,1)}, f32[2,8,512]{2,1,0:T(8,128)S(1)}, s32[2]{0:T(128)S(1)}, s32[1024]{0:T(1024)S(1)}, /*index=...) while((s32[]{:T(128)}, ...), condition=%wide.region_13.14_spmd, body=%wide.region_10.13_spmd.sunk | while | flops 1124593664 | bytes 64628996 | solution.py:80
  311.1 4.1 fusion.262
  315.2 4.2 fusion.263
  319.4 5.4 fusion.264
  327.5 4.1 fusion.262
  331.6 4.2 fusion.263
  335.8 5.4 fusion.264
  350.7 2.5 copy.80
  356.1 3.9 multiply_convert_fusion.2
  360.0 2.6 fusion.164
  363.4 2.7 fusion.105
  366.0 5.1 convolution_bitcast_fusion
  371.1 5.1 fusion.98
  376.2 4.1 multiply_reduce_fusion.2
  380.2 4.6 convolution_bitcast_fusion.1
  389.0 141.6 %while.98 = (s32[]{:T(128)}, f32[1024,8,64]{0,2,1:T(8,128)}, f32[1024,8,64]{0,2,1:T(8,128)}, bf16[2,512,8,64]{1,3,2,0:T(8,128)(2,1)}, s32[2]{0:T(128)S(1)}, /*in...) while((s32[]{:T(128)}, f32[1024,8,64]{0,2,1:T(8,128)}, ...), condition=%wide.region_24.25_spmd.clone, body=%wide.region_22.24_spmd.clone.sunk | while | flops 2745706496 | bytes 267446608 | solution.py:127
  393.0 5.8 exponential_select_fusion.4
  398.8 3.4 bitcast_add_fusion.9
  402.3 2.9 copy-done.1
  405.2 8.1 fusion.275
  413.3 22.7 %fusion.276 = bf16[2,512,8,64]{1,3,2,0:T(8,128)(2,1)} fusion(bf16[2,512,8,64]{1,3,2,0:T(8,128)(2,1)} %get-tuple-element.1065, s32[]{:T(128)S(6)} %copy.136, bf16[1024,8,64]{0,2,1:T(8,128)(2,1)} %get-tuple-element.1087, f32[8,512,1024]{2,1,0:T(8,128)} %copy-done.1, f32[8,512,1024]{2,1,0:T(8,128)} %fusion.275), kind=kOutput, calls=%fused_computation.46.clone.1 | convolution fusion | flops 557847552 | bytes 69206016 | tf_op jit(solution)/shard_map/while/body/eval_jaxpr/while/body/eval_jaxpr/hqk,khd->qhd/dot_general | solution.py:112
  436.0 23.4 %bitcast_add_fusion.8 = f32[1024,8,64]{0,2,1:T(8,128)} fusion(f32[1024,8,64]{0,2,1:T(8,128)} %get-tuple-element.1063, f32[8,512,1024]{2,1,0:T(8,128)} %copy-done.1, f32[8,512,1024]{2,1,0:T(8,128)} %fusion.275, pred[]{:T(512)S(6)} %compare.6, bf16[1024,8,64]{0,2,1:T(8,128)(2,1)} %get-tuple-element.1084, s32[]{:T(128)S(6)} %select_n.103), kind=kOutput, calls=%fused_computation.44.clone.1 | convolution fusion | flops 558896128 | bytes 71827464 | tf_op jit(solution)/shard_map/while/body/eval_jaxpr/while/body/eval_jaxpr/hqk,qhd->khd/dot_general | solution.py:115
  463.0 5.8 exponential_select_fusion.4
  468.8 6.4 bitcast_add_fusion.9
  475.8 8.1 fusion.275
  483.9 22.7 %fusion.276 = bf16[2,512,8,64]{1,3,2,0:T(8,128)(2,1)} fusion(bf16[2,512,8,64]{1,3,2,0:T(8,128)(2,1)} %get-tuple-element.1065, s32[]{:T(128)S(6)} %copy.136, bf16[1024,8,64]{0,2,1:T(8,128)(2,1)} %get-tuple-element.1087, f32[8,512,1024]{2,1,0:T(8,128)} %copy-done.1, f32[8,512,1024]{2,1,0:T(8,128)} %fusion.275), kind=kOutput, calls=%fused_computation.46.clone.1 | convolution fusion | flops 557847552 | bytes 69206016 | tf_op jit(solution)/shard_map/while/body/eval_jaxpr/while/body/eval_jaxpr/hqk,khd->qhd/dot_general | solution.py:112
  506.6 24.0 %bitcast_add_fusion.8 = f32[1024,8,64]{0,2,1:T(8,128)} fusion(f32[1024,8,64]{0,2,1:T(8,128)} %get-tuple-element.1063, f32[8,512,1024]{2,1,0:T(8,128)} %copy-done.1, f32[8,512,1024]{2,1,0:T(8,128)} %fusion.275, pred[]{:T(512)S(6)} %compare.6, bf16[1024,8,64]{0,2,1:T(8,128)(2,1)} %get-tuple-element.1084, s32[]{:T(128)S(6)} %select_n.103), kind=kOutput, calls=%fused_computation.44.clone.1 | convolution fusion | flops 558896128 | bytes 71827464 | tf_op jit(solution)/shard_map/while/body/eval_jaxpr/while/body/eval_jaxpr/hqk,qhd->khd/dot_general | solution.py:115
  530.7 2.5 copy.83
  533.5 3.4 multiply_reduce_fusion.3
  540.4 3.0 copy.105
  543.4 3.1 copy.106
  549.7 142.0 %while.99 = (s32[]{:T(128)}, f32[1024,8,64]{0,2,1:T(8,128)}, f32[1024,8,64]{0,2,1:T(8,128)}, bf16[2,512,8,64]{1,3,2,0:T(8,128)(2,1)}, s32[2]{0:T(128)S(1)}, /*in...) while((s32[]{:T(128)}, f32[1024,8,64]{0,2,1:T(8,128)}, ...), condition=%wide.region_29.30_spmd.clone, body=%wide.region_27.29_spmd.clone.sunk | while | flops 2746755584 | bytes 267450688 | solution.py:127
  553.8 5.8 exponential_select_fusion.5
  559.6 3.4 bitcast_add_fusion.11
  563.0 2.9 copy-done.2
  565.9 8.1 fusion.288
  574.1 22.7 %fusion.289 = bf16[2,512,8,64]{1,3,2,0:T(8,128)(2,1)} fusion(bf16[2,512,8,64]{1,3,2,0:T(8,128)(2,1)} %get-tuple-element.1115, s32[]{:T(128)S(6)} %copy.148, bf16[1024,8,64]{0,2,1:T(8,128)(2,1)} %get-tuple-element.1135, f32[8,512,1024]{2,1,0:T(8,128)} %copy-done.2, f32[8,512,1024]{2,1,0:T(8,128)} %fusion.288), kind=kOutput, calls=%fused_computation.78.clone.1 | convolution fusion | flops 557847552 | bytes 69206016 | tf_op jit(solution)/shard_map/while/body/eval_jaxpr/while/body/eval_jaxpr/hqk,khd->qhd/dot_general | solution.py:112
  596.7 23.4 %bitcast_add_fusion.10 = f32[1024,8,64]{0,2,1:T(8,128)} fusion(f32[1024,8,64]{0,2,1:T(8,128)} %get-tuple-element.1113, f32[8,512,1024]{2,1,0:T(8,128)} %copy-done.2, f32[8,512,1024]{2,1,0:T(8,128)} %fusion.288, pred[]{:T(512)S(6)} %compare.7, bf16[1024,8,64]{0,2,1:T(8,128)(2,1)} %get-tuple-element.1133, s32[]{:T(128)S(6)} %select_n.106), kind=kOutput, calls=%fused_computation.74.clone.1 | convolution fusion | flops 558896128 | bytes 71827464 | tf_op jit(solution)/shard_map/while/body/eval_jaxpr/while/body/eval_jaxpr/hqk,qhd->khd/dot_general | solution.py:115
  624.0 5.8 exponential_select_fusion.5
  629.8 6.4 bitcast_add_fusion.11
  636.7 8.1 fusion.288
  644.8 22.7 %fusion.289 = bf16[2,512,8,64]{1,3,2,0:T(8,128)(2,1)} fusion(bf16[2,512,8,64]{1,3,2,0:T(8,128)(2,1)} %get-tuple-element.1115, s32[]{:T(128)S(6)} %copy.148, bf16[1024,8,64]{0,2,1:T(8,128)(2,1)} %get-tuple-element.1135, f32[8,512,1024]{2,1,0:T(8,128)} %copy-done.2, f32[8,512,1024]{2,1,0:T(8,128)} %fusion.288), kind=kOutput, calls=%fused_computation.78.clone.1 | convolution fusion | flops 557847552 | bytes 69206016 | tf_op jit(solution)/shard_map/while/body/eval_jaxpr/while/body/eval_jaxpr/hqk,khd->qhd/dot_general | solution.py:112
  667.5 24.0 %bitcast_add_fusion.10 = f32[1024,8,64]{0,2,1:T(8,128)} fusion(f32[1024,8,64]{0,2,1:T(8,128)} %get-tuple-element.1113, f32[8,512,1024]{2,1,0:T(8,128)} %copy-done.2, f32[8,512,1024]{2,1,0:T(8,128)} %fusion.288, pred[]{:T(512)S(6)} %compare.7, bf16[1024,8,64]{0,2,1:T(8,128)(2,1)} %get-tuple-element.1133, s32[]{:T(128)S(6)} %select_n.106), kind=kOutput, calls=%fused_computation.74.clone.1 | convolution fusion | flops 558896128 | bytes 71827464 | tf_op jit(solution)/shard_map/while/body/eval_jaxpr/while/body/eval_jaxpr/hqk,qhd->khd/dot_general | solution.py:115
  710.5 6.6 copy.90
  717.0 7.0 copy.103
  733.6 40.9 %all-reduce.5 = f32[3072]{0:T(1024)S(1)} all-reduce(f32[3072]{0:T(1024)S(1)} %reshape.670), channel_id=6, replica_groups=mesh['dp'=8,'shard'=4] {'dp','shard'}, use_global_device_ids=true, to_apply=%region_40.41.clone | all-reduce | flops 3072 | bytes 24576
  779.4 224.7 %all-reduce.9.cloned.1.call-done = (f32[1572864]{0:T(1024)}, f32[524288]{0:T(1024)}, f32[1048576]{0:T(1024)}, f32[1048576]{0:T(1024)}) async-done(((f32[1572864]{0:T(1024)}, f32[524288]{0:T(1024)}, f32[1048576]{0:T(1024)}, f32[1048576]{0:T(1024)}), (f32[1572864]{0:T(1024)}, f32[524288]{0:T(1024)}, f32[1048576]{0:T(1024)}, f32[1048576]{0:T(1024)})) %all-reduce.9.cloned.1.call-update) | async-done | bytes 16777232
  (349 shorter events, 104.3 us)
Async XLA Ops:
  7.2 254.9 %copy-start = (bf16[1,1024,512]{2,1,0:T(8,128)(2,1)S(1)}, bf16[1,1024,512]{2,1,0:T(8,128)(2,1)}, u32[]{:S(2)}) copy-start(bf16[1,1024,512]{2,1,0:T(8,128)(2,1)} %param.29) | copy-start | bytes 3145732
  7.2 55.6 %copy-start.51 = (bf16[1,1024,512]{2,1,0:T(8,128)(2,1)S(1)}, bf16[1,1024,512]{2,1,0:T(8,128)(2,1)}, u32[]{:S(2)}) copy-start(bf16[1,1024,512]{2,1,0:T(8,128)(2,1)} %param.28) | copy-start | bytes 3145732
  7.2 61.1 %all-gather.7.cloned.1.call-start = ((), (), s32[]{:S(2)}) async-start(), calls=%async_computation.1 | async-start | bytes 1081344 | tf_op jit(solution)/shard_map/all_gather | solution.py:187
  8.9 118.0 %all-gather.9.cloned.1.call-start = ((), (), s32[]{:S(2)}) async-start(), calls=%async_computation.2 | async-start | bytes 2162688 | tf_op jit(solution)/shard_map/all_gather | solution.py:191
  10.5 175.1 %all-gather.11.cloned.1.call-start = ((), (), s32[]{:S(2)}) async-start(), calls=%async_computation.3 | async-start | bytes 2162688 | tf_op jit(solution)/shard_map/all_gather | solution.py:192
  12.1 234.8 %all-gather.5.cloned.1.call-start = ((), (), s32[]{:S(2)}) async-start(), calls=%async_computation | async-start | bytes 3244032 | tf_op jit(solution)/shard_map/all_gather | solution.py:186
  13.8 990.4 %all-reduce.9.cloned.1.call-start = ((), (), s32[]{:S(2)}) async-start(), calls=%async_computation.4 | async-start | bytes 33554432
  256.8 3.5 copy-start.39
  257.1 3.2 copy-start.40
  257.1 3.2 copy-start.52
  273.3 4.3 copy-start.29
  289.9 4.3 copy-start.29
  300.5 3.4 copy-start.3
  300.5 3.4 copy-start.10
  300.5 3.4 copy-start.57
  300.5 3.4 copy-start.35
  300.5 3.4 copy-start.49
  304.9 3.4 copy-start.6
  304.9 3.4 copy-start.65
  305.2 3.0 copy-start.70
  305.2 3.0 copy-start.72
  306.3 3.1 copy-start.5
  306.3 3.1 copy-start.11
  306.3 3.1 copy-start.56
  315.2 4.3 copy-start.31
  331.6 4.3 copy-start.31
  350.7 2.8 copy-start.7
  350.7 2.8 copy-start.55
  350.7 2.8 copy-start.66
  350.7 2.8 copy-start.73
  350.7 2.8 copy-start.78
  350.7 2.8 copy-start.93
  356.1 3.9 copy-start.46
  360.0 2.7 copy-start.12
  398.8 6.4 copy-start.1
  468.8 6.9 copy-start.1
  530.7 2.8 copy-start.67
  530.7 2.8 copy-start.8
  530.7 2.8 copy-start.16
  533.4 3.4 copy-start.21
  533.5 3.4 copy-start.71
  533.5 3.4 copy-start.74
  533.5 3.4 copy-start.79
  540.4 3.0 copy-start.25
  543.4 3.1 copy-start.54
  546.7 3.0 copy-start.4
  546.7 3.0 copy-start.58
  559.6 6.4 copy-start.2
  629.8 6.9 copy-start.2
  691.7 2.7 copy-start.43
  694.4 5.0 copy-start.23
  696.6 6.3 copy-start.18
  697.2 9.8 copy-start.17
  699.3 9.4 copy-start.27
  731.7 42.7 %copy-start.96 = (f32[96]{0:T(128)S(1)}, f32[96]{0:T(128)}, u32[]{:S(2)}) copy-start(f32[96]{0:T(128)} %param.47) | copy-start | bytes 1156
  731.8 42.7 %copy-start.97 = (f32[96]{0:T(128)S(1)}, f32[96]{0:T(128)}, u32[]{:S(2)}) copy-start(f32[96]{0:T(128)} %param.46) | copy-start | bytes 1156
  733.6 43.6 %copy-start.28 = (bf16[1024,8,64]{0,2,1:T(8,128)(2,1)S(1)}, bf16[1024,8,64]{0,2,1:T(8,128)(2,1)}, u32[]{:S(2)}) copy-start(bf16[1024,8,64]{0,2,1:T(8,128)(2,1)} %copy-done.27) | copy-start | bytes 3145732
  733.6 43.7 %copy-start.48 = (bf16[512,512]{1,0:T(8,128)(2,1)S(1)}, bf16[512,512]{1,0:T(8,128)(2,1)}, u32[]{:S(2)}) copy-start(bf16[512,512]{1,0:T(8,128)(2,1)} %slice.171) | copy-start | bytes 1572868
  777.2 226.9 %copy-start.59 = (f32[49152]{0:T(1024)S(1)}, f32[49152]{0:T(1024)}, u32[]{:S(2)}) copy-start(f32[49152]{0:T(1024)} %param.35) | copy-start | bytes 589828
  777.3 226.9 %copy-start.60 = (f32[49152]{0:T(1024)S(1)}, f32[49152]{0:T(1024)}, u32[]{:S(2)}) copy-start(f32[49152]{0:T(1024)} %param.34) | copy-start | bytes 589828
  777.3 230.3 %copy-start.61 = (f32[32768]{0:T(1024)S(1)}, f32[32768]{0:T(1024)}, u32[]{:S(2)}) copy-start(f32[32768]{0:T(1024)} %param.41) | copy-start | bytes 393220
  777.3 230.3 %copy-start.62 = (f32[32768]{0:T(1024)S(1)}, f32[32768]{0:T(1024)}, u32[]{:S(2)}) copy-start(f32[32768]{0:T(1024)} %param.40) | copy-start | bytes 393220
  777.3 230.2 %copy-start.63 = (f32[32768]{0:T(1024)S(1)}, f32[32768]{0:T(1024)}, u32[]{:S(2)}) copy-start(f32[32768]{0:T(1024)} %param.44) | copy-start | bytes 393220
  777.3 230.2 %copy-start.64 = (f32[32768]{0:T(1024)S(1)}, f32[32768]{0:T(1024)}, u32[]{:S(2)}) copy-start(f32[32768]{0:T(1024)} %param.43) | copy-start | bytes 393220
  (45 other events, 71.7 us)
Sparse Core Ops, SparseCore 0:
  11.5 56.7 all-gather.6
  71.7 55.1 all-gather.8
  130.4 55.2 all-gather.10
  189.0 57.8 all-gather.4
  724.3 279.8 all-reduce.8
where the time goes:
time: 1030 us; the launch traced here: 1020 us
  waiting for transfers between devices  396 us (38%)
  matrix products  361 us (35%)
  local copies, waits for them, and re-layouts  91.7 us (9%)
  blocking collectives  83 us (8%)
  other arithmetic  46.3 us (4%)
  loops' own time  23.1 us (2%)
  between operations  15.5 us (2%)
    unnamed x6, waiting for transfers between devices  225 us
    dot_general x4, matrix products, one_block(): jnp.einsum('hqk,qhd->khd', grad_scores, q_block, preferred_element_type=j...  94.7 us
    dot_general x4, matrix products, one_block(): jnp.einsum('hqk,khd->qhd', grad_scores, k_row, preferred_element_type=jnp...  90.7 us
    unnamed x2, blocking collectives  83 us
    all_gather x1, waiting for transfers between devices, body(): lax.all_gather(inward_low, ('dp', 'shard'), axis=0, tiled=True)  56.9 us
    all_gather x1, waiting for transfers between devices, body(): lax.all_gather(expand_low, ('dp', 'shard'), axis=0, tiled=True)  55.1 us
    all_gather x1, waiting for transfers between devices, body(): lax.all_gather(shrink_low, ('dp', 'shard'), axis=0, tiled=True)  54.6 us
    dot_general x8, matrix products, one_block(): jnp.einsum('qhd,khd->hqk', q_block, k_row, preferred_element_type=jnp.flo...  39.5 us
  transfers between devices with their start and end apart: 5, of which 5 were waited for; matrix products, arithmetic and copies ran while one was open for 4% of the time, Pallas kernels for 0%

commit v1 on v0

--- a/solution.py
+++ b/solution.py
@@ -13,6 +13,18 @@
 learn_rate = 0.001
 beta_one = 0.9
 beta_two = 0.999
+
+
+def doubled_up(x, axis, dim):
+    ways, here, turn = (lax.axis_size(axis), lax.axis_index(axis), x.shape[dim])
+    line, have = (x, 1)
+    while have < ways:
+        line = jnp.concatenate(
+            [line, lax.ppermute(line, axis, [(d, (d - have) % ways) for d in range(ways)])],
+            axis=dim,
+        )
+        have = 2 * have
+    return jnp.roll(line, here * turn, axis=dim)
 
 
 def matmul(left_mat, right_mat):
@@ -188,7 +200,7 @@
         lax.all_gather(norms_low, ("dp", "shard"), axis=0, tiled=True),
     )
     expand_all, shrink_all = (
-        lax.all_gather(expand_low, ("dp", "shard"), axis=0, tiled=True),
+        doubled_up(expand_low, ("dp", "shard"), 0),
         lax.all_gather(shrink_low, ("dp", "shard"), axis=0, tiled=True),
     )
     w_in, w_out, w_up, w_down, gains, biases = unpack(

time: 1030 us -> 1060 us (1.029)
  local copies, waits for them, and re-layouts: 91.7 us -> 110 us
  starting transfers between devices: 0.21 us -> 17.4 us
    ppermute x0 -> x5, waiting for transfers between devices: none -> 56 us  [doubled_up(): lax.ppermute(line, axis, [(d, (d - have) % ways) for d in range(ways)])]
    all_gather x1, waiting for transfers between devices: 54.6 us -> 10.2 us  [body(): lax.all_gather(shrink_low, ('dp', 'shard'), axis=0, tiled=True)]
    ppermute x0 -> x5, starting transfers between devices: none -> 17.2 us  [doubled_up(): lax.ppermute(line, axis, [(d, (d - have) % ways) for d in range(ways)])]
    unnamed x198 -> x216, local copies, waits for them, and re-layouts: 31.5 us -> 40.5 us
  transfers between devices with their start and end apart: 5 -> 10, of which waited for: 5 -> 8; matrix products, arithmetic and copies ran while one was open for 4% -> 5% of each run, Pallas kernels for 0% -> 0%
where the time goes in v1:
time: 1060 us; the launch traced here: 1050 us
  waiting for transfers between devices  403 us (38%)
  matrix products  361 us (34%)
  local copies, waits for them, and re-layouts  110 us (10%)
  blocking collectives  78 us (7%)
  other arithmetic  46.4 us (4%)
  loops' own time  23.1 us (2%)
  starting transfers between devices  17.4 us (2%)
  between operations  15.6 us (1%)
    unnamed x6, waiting for transfers between devices  225 us
    dot_general x4, matrix products, one_block(): jnp.einsum('hqk,qhd->khd', grad_scores, q_block, preferred_element_type=j...  94.5 us
    dot_general x4, matrix products, one_block(): jnp.einsum('hqk,khd->qhd', grad_scores, k_row, preferred_element_type=jnp...  90.7 us
    unnamed x2, blocking collectives  78 us
    all_gather x1, waiting for transfers between devices, body(): lax.all_gather(inward_low, ('dp', 'shard'), axis=0, tiled=True)  57.1 us
    ppermute x5, waiting for transfers between devices, doubled_up(): lax.ppermute(line, axis, [(d, (d - have) % ways) for d in range(ways)])  56 us
    all_gather x1, waiting for transfers between devices, body(): lax.all_gather(expand_low, ('dp', 'shard'), axis=0, tiled=True)  54.4 us
    unnamed x216, local copies, waits for them, and re-layouts  40.5 us
  transfers between devices with their start and end apart: 10, of which 8 were waited for; matrix products, arithmetic and copies ran while one was open for 5% of the time, Pallas kernels for 0%

profile of v1, /device:TPU:0, one launch (start us, length us, event | category | flops | bytes accessed | tf_op | source)
XLA Modules:
  0.0 1054.2 jit_solution(18210364870356924483)
XLA Ops:
  12.2 6.4 collective-permute-start
  25.0 37.1 %all-reduce = bf16[3072]{0:T(1024)(128)(2,1)S(1)} all-reduce(bf16[3072]{0:T(1024)(128)(2,1)S(1)} %dynamic-update-slice), channel_id=1, replica_groups=mesh['dp'=8,'shard'=4] {'dp','shard'}, use_global_device_ids=true, to_apply=%add | all-reduce | flops 3072 | bytes 12288
  67.1 3.7 collective-permute-start.1
  76.8 3.3 collective-permute-done.2
  83.2 10.4 collective-permute-done.3
  104.2 40.2 %collective-permute-done.4 = bf16[524288]{0:T(1024)(128)(2,1)S(1)} collective-permute-done((bf16[524288]{0:T(1024)(128)(2,1)}, bf16[524288]{0:T(1024)(128)(2,1)S(1)}, u32[]{:S(2)}, u32[]{:S(2)}) %collective-permute-start.4) | collective-permute-done | bytes 1048608 | tf_op jit(solution)/shard_map/ppermute | solution.py:23
  154.0 10.2 all-gather.9.cloned.1.call-done
  164.1 4.3 reshape.658
  168.5 54.4 %all-gather.11.cloned.1.call-done = bf16[1048576]{0:T(1024)(128)(2,1)} async-done(((bf16[32768]{0:T(1024)(128)(2,1)}), bf16[1048576]{0:T(1024)(128)(2,1)}) %all-gather.11.cloned.1.call-update) | async-done | bytes 2097168 | tf_op jit(solution)/shard_map/all_gather | solution.py:246
  222.9 4.1 reshape.660
  227.0 57.1 %all-gather.5.cloned.1.call-done = bf16[1572864]{0:T(1024)(128)(2,1)} async-done(((bf16[49152]{0:T(1024)(128)(2,1)}), bf16[1572864]{0:T(1024)(128)(2,1)}) %all-gather.5.cloned.1.call-update) | async-done | bytes 3145744 | tf_op jit(solution)/shard_map/all_gather | solution.py:198
  284.1 3.0 fusion.159
  294.3 3.2 convolution_convert_fusion.7
  304.2 33.5 %while.96 = (s32[]{:T(128)}, bf16[2,512,8,64]{1,3,2,0:T(8,128)(2,1)}, f32[2,8,512]{2,1,0:T(8,128)S(1)}, s32[2]{0:T(128)S(1)}, s32[1024]{0:T(1024)S(1)}, /*index=...) while((s32[]{:T(128)}, ...), condition=%wide.region_5.6_spmd, body=%wide.region_2.5_spmd.sunk | while | flops 1125642752 | bytes 64633092 | solution.py:92
  306.4 4.1 fusion.257
  310.5 4.2 fusion.258
  314.7 5.4 fusion.259
  323.0 4.1 fusion.257
  327.1 4.2 fusion.258
  331.4 5.4 fusion.259
  337.8 3.1 copy.79
  346.6 41.3 %while.97 = (s32[]{:T(128)}, bf16[2,512,8,64]{1,3,2,0:T(8,128)(2,1)}, f32[2,8,512]{2,1,0:T(8,128)S(1)}, s32[2]{0:T(128)S(1)}, s32[1024]{0:T(1024)S(1)}, /*index=...) while((s32[]{:T(128)}, ...), condition=%wide.region_13.14_spmd, body=%wide.region_10.13_spmd.sunk | while | flops 1124593664 | bytes 64628996 | solution.py:92
  348.3 4.1 fusion.262
  352.4 4.2 fusion.263
  356.6 5.4 fusion.264
  364.7 4.1 fusion.262
  368.8 4.2 fusion.263
  373.0 5.4 fusion.264
  393.3 3.9 multiply_convert_fusion.2
  403.2 5.1 convolution_bitcast_fusion
  408.3 5.0 fusion.98
  413.3 4.6 convolution_bitcast_fusion.1
  417.9 4.1 multiply_reduce_fusion.2
  426.3 141.6 %while.98 = (s32[]{:T(128)}, f32[1024,8,64]{0,2,1:T(8,128)}, f32[1024,8,64]{0,2,1:T(8,128)}, bf16[2,512,8,64]{1,3,2,0:T(8,128)(2,1)}, s32[2]{0:T(128)S(1)}, /*in...) while((s32[]{:T(128)}, f32[1024,8,64]{0,2,1:T(8,128)}, ...), condition=%wide.region_24.25_spmd.clone, body=%wide.region_22.24_spmd.clone.sunk | while | flops 2745706496 | bytes 267446608 | solution.py:139
  430.3 5.8 exponential_select_fusion.4
  436.1 3.5 bitcast_add_fusion.9
  439.5 2.9 copy-done.1
  442.5 8.2 fusion.275
  450.6 22.7 %fusion.276 = bf16[2,512,8,64]{1,3,2,0:T(8,128)(2,1)} fusion(bf16[2,512,8,64]{1,3,2,0:T(8,128)(2,1)} %get-tuple-element.1075, s32[]{:T(128)S(6)} %copy.151, bf16[1024,8,64]{0,2,1:T(8,128)(2,1)} %get-tuple-element.1097, f32[8,512,1024]{2,1,0:T(8,128)} %copy-done.1, f32[8,512,1024]{2,1,0:T(8,128)} %fusion.275), kind=kOutput, calls=%fused_computation.46.clone.1 | convolution fusion | flops 557847552 | bytes 69206016 | tf_op jit(solution)/shard_map/while/body/eval_jaxpr/while/body/eval_jaxpr/hqk,khd->qhd/dot_general | solution.py:124
  473.3 23.3 %bitcast_add_fusion.8 = f32[1024,8,64]{0,2,1:T(8,128)} fusion(f32[1024,8,64]{0,2,1:T(8,128)} %get-tuple-element.1073, f32[8,512,1024]{2,1,0:T(8,128)} %copy-done.1, f32[8,512,1024]{2,1,0:T(8,128)} %fusion.275, pred[]{:T(512)S(6)} %compare.7, bf16[1024,8,64]{0,2,1:T(8,128)(2,1)} %get-tuple-element.1094, s32[]{:T(128)S(6)} %select_n.118), kind=kOutput, calls=%fused_computation.44.clone.1 | convolution fusion | flops 558896128 | bytes 71827464 | tf_op jit(solution)/shard_map/while/body/eval_jaxpr/while/body/eval_jaxpr/hqk,qhd->khd/dot_general | solution.py:127
  500.3 5.8 exponential_select_fusion.4
  506.1 6.4 bitcast_add_fusion.9
  513.0 8.2 fusion.275
  521.2 22.7 %fusion.276 = bf16[2,512,8,64]{1,3,2,0:T(8,128)(2,1)} fusion(bf16[2,512,8,64]{1,3,2,0:T(8,128)(2,1)} %get-tuple-element.1075, s32[]{:T(128)S(6)} %copy.151, bf16[1024,8,64]{0,2,1:T(8,128)(2,1)} %get-tuple-element.1097, f32[8,512,1024]{2,1,0:T(8,128)} %copy-done.1, f32[8,512,1024]{2,1,0:T(8,128)} %fusion.275), kind=kOutput, calls=%fused_computation.46.clone.1 | convolution fusion | flops 557847552 | bytes 69206016 | tf_op jit(solution)/shard_map/while/body/eval_jaxpr/while/body/eval_jaxpr/hqk,khd->qhd/dot_general | solution.py:124
  543.8 23.9 %bitcast_add_fusion.8 = f32[1024,8,64]{0,2,1:T(8,128)} fusion(f32[1024,8,64]{0,2,1:T(8,128)} %get-tuple-element.1073, f32[8,512,1024]{2,1,0:T(8,128)} %copy-done.1, f32[8,512,1024]{2,1,0:T(8,128)} %fusion.275, pred[]{:T(512)S(6)} %compare.7, bf16[1024,8,64]{0,2,1:T(8,128)(2,1)} %get-tuple-element.1094, s32[]{:T(128)S(6)} %select_n.118), kind=kOutput, calls=%fused_computation.44.clone.1 | convolution fusion | flops 558896128 | bytes 71827464 | tf_op jit(solution)/shard_map/while/body/eval_jaxpr/while/body/eval_jaxpr/hqk,qhd->khd/dot_general | solution.py:127
  570.7 3.4 multiply_reduce_fusion.3
  577.7 3.0 copy.105
  580.7 3.1 copy.106
  586.9 142.1 %while.99 = (s32[]{:T(128)}, f32[1024,8,64]{0,2,1:T(8,128)}, f32[1024,8,64]{0,2,1:T(8,128)}, bf16[2,512,8,64]{1,3,2,0:T(8,128)(2,1)}, s32[2]{0:T(128)S(1)}, /*in...) while((s32[]{:T(128)}, f32[1024,8,64]{0,2,1:T(8,128)}, ...), condition=%wide.region_29.30_spmd.clone, body=%wide.region_27.29_spmd.clone.sunk | while | flops 2746755584 | bytes 267450688 | solution.py:139
  591.0 5.8 exponential_select_fusion.5
  596.8 3.4 bitcast_add_fusion.11
  600.2 3.0 copy-done.2
  603.2 8.2 fusion.288
  611.3 22.7 %fusion.289 = bf16[2,512,8,64]{1,3,2,0:T(8,128)(2,1)} fusion(bf16[2,512,8,64]{1,3,2,0:T(8,128)(2,1)} %get-tuple-element.1125, s32[]{:T(128)S(6)} %copy.163, bf16[1024,8,64]{0,2,1:T(8,128)(2,1)} %get-tuple-element.1145, f32[8,512,1024]{2,1,0:T(8,128)} %copy-done.2, f32[8,512,1024]{2,1,0:T(8,128)} %fusion.288), kind=kOutput, calls=%fused_computation.78.clone.1 | convolution fusion | flops 557847552 | bytes 69206016 | tf_op jit(solution)/shard_map/while/body/eval_jaxpr/while/body/eval_jaxpr/hqk,khd->qhd/dot_general | solution.py:124
  634.0 23.3 %bitcast_add_fusion.10 = f32[1024,8,64]{0,2,1:T(8,128)} fusion(f32[1024,8,64]{0,2,1:T(8,128)} %get-tuple-element.1123, f32[8,512,1024]{2,1,0:T(8,128)} %copy-done.2, f32[8,512,1024]{2,1,0:T(8,128)} %fusion.288, pred[]{:T(512)S(6)} %compare.8, bf16[1024,8,64]{0,2,1:T(8,128)(2,1)} %get-tuple-element.1143, s32[]{:T(128)S(6)} %select_n.121), kind=kOutput, calls=%fused_computation.74.clone.1 | convolution fusion | flops 558896128 | bytes 71827464 | tf_op jit(solution)/shard_map/while/body/eval_jaxpr/while/body/eval_jaxpr/hqk,qhd->khd/dot_general | solution.py:127
  661.2 5.8 exponential_select_fusion.5
  667.0 6.5 bitcast_add_fusion.11
  674.0 8.2 fusion.288
  682.1 22.7 %fusion.289 = bf16[2,512,8,64]{1,3,2,0:T(8,128)(2,1)} fusion(bf16[2,512,8,64]{1,3,2,0:T(8,128)(2,1)} %get-tuple-element.1125, s32[]{:T(128)S(6)} %copy.163, bf16[1024,8,64]{0,2,1:T(8,128)(2,1)} %get-tuple-element.1145, f32[8,512,1024]{2,1,0:T(8,128)} %copy-done.2, f32[8,512,1024]{2,1,0:T(8,128)} %fusion.288), kind=kOutput, calls=%fused_computation.78.clone.1 | convolution fusion | flops 557847552 | bytes 69206016 | tf_op jit(solution)/shard_map/while/body/eval_jaxpr/while/body/eval_jaxpr/hqk,khd->qhd/dot_general | solution.py:124
  704.8 23.9 %bitcast_add_fusion.10 = f32[1024,8,64]{0,2,1:T(8,128)} fusion(f32[1024,8,64]{0,2,1:T(8,128)} %get-tuple-element.1123, f32[8,512,1024]{2,1,0:T(8,128)} %copy-done.2, f32[8,512,1024]{2,1,0:T(8,128)} %fusion.288, pred[]{:T(512)S(6)} %compare.8, bf16[1024,8,64]{0,2,1:T(8,128)(2,1)} %get-tuple-element.1143, s32[]{:T(128)S(6)} %select_n.121), kind=kOutput, calls=%fused_computation.74.clone.1 | convolution fusion | flops 558896128 | bytes 71827464 | tf_op jit(solution)/shard_map/while/body/eval_jaxpr/while/body/eval_jaxpr/hqk,qhd->khd/dot_general | solution.py:127
  747.7 6.7 copy.90
  754.4 7.1 copy.103
  771.0 40.9 %all-reduce.5 = f32[3072]{0:T(1024)S(1)} all-reduce(f32[3072]{0:T(1024)S(1)} %reshape.673), channel_id=6, replica_groups=mesh['dp'=8,'shard'=4] {'dp','shard'}, use_global_device_ids=true, to_apply=%region_40.41.clone | all-reduce | flops 3072 | bytes 24576
  816.8 225.0 %all-reduce.9.cloned.1.call-done = (f32[1572864]{0:T(1024)}, f32[524288]{0:T(1024)}, f32[1048576]{0:T(1024)}, f32[1048576]{0:T(1024)}) async-done(((f32[1572864]{0:T(1024)}, f32[524288]{0:T(1024)}, f32[1048576]{0:T(1024)}, f32[1048576]{0:T(1024)}), (f32[1572864]{0:T(1024)}, f32[524288]{0:T(1024)}, f32[1048576]{0:T(1024)}, f32[1048576]{0:T(1024)})) %all-reduce.9.cloned.1.call-update) | async-done | bytes 16777232
  (384 shorter events, 141.7 us)
Async XLA Ops:
  7.2 292.1 %copy-start = (bf16[1,1024,512]{2,1,0:T(8,128)(2,1)S(1)}, bf16[1,1024,512]{2,1,0:T(8,128)(2,1)}, u32[]{:S(2)}) copy-start(bf16[1,1024,512]{2,1,0:T(8,128)(2,1)} %param.29) | copy-start | bytes 3145732
  7.2 55.5 %copy-start.53 = (bf16[1,1024,512]{2,1,0:T(8,128)(2,1)S(1)}, bf16[1,1024,512]{2,1,0:T(8,128)(2,1)}, u32[]{:S(2)}) copy-start(bf16[1,1024,512]{2,1,0:T(8,128)(2,1)} %param.30) | copy-start | bytes 3145732
  7.2 90.4 %all-gather.7.cloned.1.call-start = ((), (), s32[]{:S(2)}) async-start(), calls=%async_computation.1 | async-start | bytes 1081344 | tf_op jit(solution)/shard_map/all_gather | solution.py:199
  8.9 155.3 %all-gather.9.cloned.1.call-start = ((), (), s32[]{:S(2)}) async-start(), calls=%async_computation.2 | async-start | bytes 2162688 | tf_op jit(solution)/shard_map/all_gather | solution.py:204
  10.5 212.4 %all-gather.11.cloned.1.call-start = ((), (), s32[]{:S(2)}) async-start(), calls=%async_computation.3 | async-start | bytes 2162688 | tf_op jit(solution)/shard_map/all_gather | solution.py:246
  12.1 272.0 %all-gather.5.cloned.1.call-start = ((), (), s32[]{:S(2)}) async-start(), calls=%async_computation | async-start | bytes 3244032 | tf_op jit(solution)/shard_map/all_gather | solution.py:198
  12.2 54.9 %collective-permute-start = (bf16[32768]{0:T(1024)(128)(2,1)}, bf16[32768]{0:T(1024)(128)(2,1)S(1)}, u32[]{:S(2)}, u32[]{:S(2)}) collective-permute-start(bf16[32768]{0:T(1024)(128)(2,1)} %get-tuple-element.683), channel_id=1, source_target_pairs={{0,31},{1,0},{2,1},{3,2},{4,3},{5,4},{6,5},{7,6},{8,7},{9,8},{10,9... | collective-permute-start | bytes 196616 | tf_op jit(solution)/shard_map/ppermute | solution.py:23
  20.2 1021.6 %all-reduce.9.cloned.1.call-start = ((), (), s32[]{:S(2)}) async-start(), calls=%async_computation.4 | async-start | bytes 33554432
  62.7 4.4 copy-start.36
  64.0 6.7 copy-start.92
  67.1 6.5 collective-permute-start.1
  73.6 6.4 collective-permute-start.2
  80.1 13.5 %collective-permute-start.3 = (bf16[262144]{0:T(1024)(128)(2,1)S(1)}, bf16[262144]{0:T(1024)(128)(2,1)S(1)}, u32[]{:S(2)}, u32[]{:S(2)}) collective-permute-start(bf16[262144]{0:T(1024)(128)(2,1)S(1)} %pad_maximum_fusion.1), channel_id=1, source_target_pairs={{0,24},{1,25},{2,26},{3,27},{4,28},{5,29},{6,30},{7,31},{8,0},{9,1... | collective-permute-start | bytes 1572872 | tf_op jit(solution)/shard_map/ppermute | solution.py:23
  95.5 49.0 %collective-permute-start.4 = (bf16[524288]{0:T(1024)(128)(2,1)}, bf16[524288]{0:T(1024)(128)(2,1)S(1)}, u32[]{:S(2)}, u32[]{:S(2)}) collective-permute-start(bf16[524288]{0:T(1024)(128)(2,1)} %copy-done.93), channel_id=1, source_target_pairs={{0,16},{1,17},{2,18},{3,19},{4,20},{5,21},{6,22},{7,23},{8,24},{9,... | collective-permute-start | bytes 3145736 | tf_op jit(solution)/shard_map/ppermute | solution.py:23
  294.0 3.5 copy-start.40
  294.3 3.2 copy-start.41
  294.3 3.2 copy-start.54
  310.5 4.3 copy-start.29
  327.1 4.3 copy-start.29
  337.7 3.4 copy-start.3
  337.7 3.4 copy-start.10
  337.7 3.4 copy-start.59
  337.7 3.4 copy-start.35
  337.7 3.4 copy-start.51
  342.1 3.3 copy-start.6
  342.2 3.3 copy-start.67
  342.5 3.0 copy-start.72
  342.5 3.0 copy-start.74
  343.6 3.0 copy-start.5
  343.6 3.0 copy-start.11
  343.6 3.0 copy-start.58
  352.4 4.3 copy-start.31
  368.8 4.3 copy-start.31
  387.9 2.8 copy-start.7
  387.9 2.8 copy-start.57
  387.9 2.8 copy-start.68
  393.3 3.9 copy-start.47
  413.3 4.6 copy-start.46
  436.1 6.4 copy-start.1
  506.1 6.9 copy-start.1
  570.7 3.5 copy-start.21
  570.7 3.4 copy-start.73
  570.7 3.4 copy-start.76
  570.7 3.4 copy-start.81
  577.7 3.0 copy-start.25
  580.7 3.1 copy-start.56
  583.9 3.0 copy-start.4
  584.0 3.0 copy-start.60
  596.8 6.4 copy-start.2
  667.0 6.9 copy-start.2
  731.7 5.0 copy-start.23
  733.9 6.3 copy-start.18
  734.5 9.8 copy-start.17
  736.6 9.4 copy-start.27
  769.1 42.8 %copy-start.100 = (f32[96]{0:T(128)S(1)}, f32[96]{0:T(128)}, u32[]{:S(2)}) copy-start(f32[96]{0:T(128)} %param.47) | copy-start | bytes 1156
  769.1 42.7 %copy-start.101 = (f32[96]{0:T(128)S(1)}, f32[96]{0:T(128)}, u32[]{:S(2)}) copy-start(f32[96]{0:T(128)} %param.46) | copy-start | bytes 1156
  771.0 43.7 %copy-start.28 = (bf16[1024,8,64]{0,2,1:T(8,128)(2,1)S(1)}, bf16[1024,8,64]{0,2,1:T(8,128)(2,1)}, u32[]{:S(2)}) copy-start(bf16[1024,8,64]{0,2,1:T(8,128)(2,1)} %copy-done.27) | copy-start | bytes 3145732
  771.0 43.7 %copy-start.50 = (bf16[512,512]{1,0:T(8,128)(2,1)S(1)}, bf16[512,512]{1,0:T(8,128)(2,1)}, u32[]{:S(2)}) copy-start(bf16[512,512]{1,0:T(8,128)(2,1)} %slice.171) | copy-start | bytes 1572868
  814.6 227.2 %copy-start.61 = (f32[49152]{0:T(1024)S(1)}, f32[49152]{0:T(1024)}, u32[]{:S(2)}) copy-start(f32[49152]{0:T(1024)} %param.35) | copy-start | bytes 589828
  814.6 227.2 %copy-start.62 = (f32[49152]{0:T(1024)S(1)}, f32[49152]{0:T(1024)}, u32[]{:S(2)}) copy-start(f32[49152]{0:T(1024)} %param.34) | copy-start | bytes 589828
  814.7 230.6 %copy-start.63 = (f32[32768]{0:T(1024)S(1)}, f32[32768]{0:T(1024)}, u32[]{:S(2)}) copy-start(f32[32768]{0:T(1024)} %param.41) | copy-start | bytes 393220
  814.7 230.5 %copy-start.64 = (f32[32768]{0:T(1024)S(1)}, f32[32768]{0:T(1024)}, u32[]{:S(2)}) copy-start(f32[32768]{0:T(1024)} %param.40) | copy-start | bytes 393220
  814.7 230.5 %copy-start.65 = (f32[32768]{0:T(1024)S(1)}, f32[32768]{0:T(1024)}, u32[]{:S(2)}) copy-start(f32[32768]{0:T(1024)} %param.44) | copy-start | bytes 393220
  814.7 230.5 %copy-start.66 = (f32[32768]{0:T(1024)S(1)}, f32[32768]{0:T(1024)}, u32[]{:S(2)}) copy-start(f32[32768]{0:T(1024)} %param.43) | copy-start | bytes 393220
  (54 other events, 94.6 us)
Sparse Core Ops, SparseCore 0:
  11.5 56.5 all-gather.6
  71.6 92.5 all-gather.8
  167.6 55.2 all-gather.10
  226.2 57.8 all-gather.4
  761.6 280.1 all-reduce.8
